TPU v7x, 256 devices: a whole 4x4x8 slice. The times are simulated.
256 devices in a mesh: ctx: 64 (over z, x, core), head: 4 (over y).
Axes of the slice: x: 4, y: 4, z: 8, core: 2. Of those that a mesh axis runs over, the one named last changes fastest.
Arguments:
- queries: float32 [16384, 4096], P('ctx', 'head'), may hold values from -48 to 48
- keys: float32 [16384, 4096], P('ctx', 'head'), may hold values from -48 to 48
- values: float32 [16384, 4096], P('ctx', 'head'), may hold values from -8 to 8
- query_map: float32 [32, 128, 128], P('head'), may hold values from -2 to 2
- key_map: float32 [32, 128, 128], P('head'), may hold values from -2 to 2
- out_weight: float32 [4096, 4096], P(None, ('ctx', 'head')), may hold values from -0.09375 to 0.09375
- residual: float32 [16384, 4096], P('ctx', 'head'), may hold values from -1.5 to 1.5
Outputs:
- layer_out: float32 [16384, 4096], P('ctx', 'head')
All inputs are finite; a program needn't handle non-finite values.
Results may differ from a plain program's by a relative error of at most 0.0001.
Values sent between devices are 32-bit elements; how exact they have to be, the bound alone decides.
A program may use at most 192 MiB of HBM per device.

v0:
```python
import jax
import jax.numpy as jnp
from jax import lax
from jax.sharding import PartitionSpec as P

HIGH = lax.Precision.HIGHEST


def carried_in(part, axis, combine, identity):
    place = lax.axis_index(axis)
    gathered = jax.tree.map(lambda a: lax.all_gather(a, axis), part)
    state = jax.tree.map(lambda a, e: jnp.zeros_like(a) + jnp.asarray(e, a.dtype), part, identity)

    def one(step, state):
        return combine(
            state, jax.tree.map(lambda a: lax.dynamic_index_in_dim(a, step, 0, False), gathered)
        )

    return lax.fori_loop(0, place, one, state)


def feature_map(inputs, weights):
    scores = jnp.einsum("nhd,hdf->hnf", inputs, weights, precision=HIGH)
    return jnp.concatenate(
        [jax.nn.softmax(scores, axis=-1), jax.nn.softmax(-scores, axis=-1)], axis=-1
    )


def add_pair(earlier, later):
    return (earlier[0] + later[0], earlier[1] + later[1])


def body(queries, keys, values, query_map, key_map, out_weight, residual):
    rows = queries.shape[0]
    heads_here, head_size, _ = query_map.shape
    width = heads_here * head_size
    shaped = (rows, heads_here, head_size)
    query_feat = feature_map(queries.reshape(shaped), query_map)
    key_feat = feature_map(keys.reshape(shaped), key_map)
    value_heads = values.reshape(shaped).transpose(1, 0, 2)
    local_state = jnp.einsum("hkf,hkd->hfd", key_feat, value_heads, precision=HIGH)
    local_norm = jnp.sum(key_feat, axis=1)
    zero_pair = (jnp.zeros_like(local_state), jnp.zeros_like(local_norm))
    prior_state, prior_norm = carried_in((local_state, local_norm), "ctx", add_pair, zero_pair)
    causal = jnp.tril(jnp.ones((rows, rows), jnp.float32))
    weights = jnp.einsum("hqf,hkf->hqk", query_feat, key_feat, precision=HIGH) * causal
    numer = jnp.einsum("hqk,hkd->hqd", weights, value_heads, precision=HIGH)
    numer = numer + jnp.einsum("hqf,hfd->hqd", query_feat, prior_state, precision=HIGH)
    denom = jnp.sum(weights, axis=-1) + jnp.einsum(
        "hqf,hf->hq", query_feat, prior_norm, precision=HIGH
    )
    mixed = (numer / denom[..., None]).transpose(1, 0, 2).reshape(rows, width)
    own_rows = lax.all_to_all(out_weight, "head", split_axis=0, concat_axis=1, tiled=True)
    partial_value = jnp.dot(
        mixed,
        lax.all_gather(own_rows, "ctx", axis=1, tiled=True),
        precision=HIGH,
        preferred_element_type=jnp.float32,
    )
    projected = lax.psum_scatter(partial_value, "head", scatter_dimension=1, tiled=True)
    return residual + projected


def solution(mesh):
    placed = (
        P("ctx", "head"),
        P("ctx", "head"),
        P("ctx", "head"),
        P("head", None, None),
        P("head", None, None),
        P(None, ("ctx", "head")),
        P("ctx", "head"),
    )
    return jax.shard_map(
        body, mesh=mesh, in_specs=placed, out_specs=P("ctx", "head"), check_vma=False
    )
```

profile of v0, /device:TPU:1, one launch (start us, length us, event | category | flops | bytes accessed | tf_op | source)
XLA Modules:
  0.0 486.4 jit_solution(5535288748645154746)
XLA Ops:
  6.5 1.2 copy-done
  7.8 2.1 fusion.29
  9.9 1.1 fusion.46
  11.0 1.1 fusion.47
  12.1 0.2 broadcast_divide_fusion
  12.3 1.3 copy-done.6
  13.6 3.0 fusion.24
  16.6 0.0 all-gather.5.cloned.1.call-start
  16.7 10.4 %all_to_all.19 = f32[4,1024,16]{1,2,0:T(8,128)} all-to-all(f32[4,1024,16]{1,2,0:T(8,128)S(1)} %bitcast.68), channel_id=1, replica_groups=mesh['ctx'=64,'head'=4] {'head'}, dimensions={0} | all-to-all | bytes 524288 | tf_op jit(solution)/shard_map/all_to_all | solution.py:53
  27.1 0.0 reduce-scatter.2.cloned.1.call-start
  27.2 2.5 copy.70
  29.8 0.3 fusion.23
  30.1 60.9 %all-gather.1 = f32[512,256]{1,0:T(8,128)} all-gather(f32[8,256]{1,0:T(8,128)S(1)} %fusion.23), channel_id=3, replica_groups=mesh['ctx'=64,'head'=4] {'ctx'}, dimensions={0}, use_global_device_ids=true | all-gather | bytes 532480 | tf_op jit(solution)/shard_map/all_gather | solution.py:11
  91.1 1.1 fusion.32
  92.2 1.1 fusion.48
  93.3 1.1 fusion.49
  94.4 0.2 broadcast_divide_fusion.2
  94.6 1.0 copy-done.1
  95.6 0.3 copy-done.4
  96.0 4.8 multiply_reduce_fusion
  100.8 157.3 %all-gather.7.cloned.1.call-done = f32[512,256,128]{2,1,0:T(8,128)} async-done(((f32[8,256,128]{2,1,0:T(8,128)}), f32[512,256,128]{2,1,0:T(8,128)}) %all-gather.7.cloned.1.call-update) | async-done | bytes 67108880 | tf_op jit(solution)/shard_map/all_gather | solution.py:11
  258.1 0.1 broadcast_in_dim.11
  258.2 2.4 while.12
  258.4 1.5 bitcast_add_fusion.5
  259.9 0.7 bitcast_add_fusion.6
  260.6 2.5 fusion.26
  263.1 2.0 fusion.27
  265.2 2.2 fusion.20
  267.4 89.8 %all-gather.5.cloned.1.call-done = f32[1024,4096]{0,1:T(8,128)} async-done(((f32[1024,64]{0,1:T(8,128)}), f32[1024,4096]{0,1:T(8,128)}) %all-gather.5.cloned.1.call-update) | async-done | bytes 16777232 | tf_op jit(solution)/shard_map/all_gather | solution.py:56
  357.2 30.4 %fusion.50 = f32[256,4096]{1,0:T(8,128)} fusion(f32[256,1024]{0,1:T(8,128)S(1)} %bitcast.64, f32[1024,4096]{0,1:T(8,128)} %all-gather.5.cloned.1.call-done), kind=kOutput, calls=%fused_computation.59 | convolution fusion | flops 12884901888 | bytes 22020096 | tf_op jit(solution)/shard_map/dot_general | solution.py:54
  387.6 89.9 %reduce-scatter.2.cloned.1.call-done = f32[256,1024]{1,0:T(8,128)} async-done(((f32[256,4096]{1,0:T(8,128)}), f32[256,1024]{1,0:T(8,128)}) %reduce-scatter.2.cloned.1.call-update) | async-done | bytes 1048592 | tf_op jit(solution)/shard_map/reduce_scatter | solution.py:60
  477.6 2.3 add.38
  (28 shorter events, 0.1 us)
Async XLA Ops:
  6.5 1.2 copy-start
  6.5 251.6 %all-gather.7.cloned.1.call-start = ((), (), s32[]{:S(2)}) async-start(), calls=%async_computation.4 | async-start | bytes 68157440 | tf_op jit(solution)/shard_map/all_gather | solution.py:11
  12.1 1.5 copy-start.6
  12.3 17.4 %copy-start.3 = (f32[8,256,128]{1,2,0:T(8,128)}, f32[8,256,128]{1,2,0:T(8,128)S(1)}, u32[]{:S(2)}) copy-start(f32[8,256,128]{1,2,0:T(8,128)S(1)} %get-tuple-element.64) | copy-start | bytes 3145732
  13.6 3.0 copy-start.11
  16.6 340.6 %all-gather.5.cloned.1.call-start = ((), (), s32[]{:S(2)}) async-start(), calls=%async_computation.2 | async-start | bytes 17039360 | tf_op jit(solution)/shard_map/all_gather | solution.py:56
  27.1 450.4 %reduce-scatter.2.cloned.1.call-start = ((), (), s32[]{:S(2)}) async-start(), calls=%async_computation.3 | async-start | bytes 5242880 | tf_op jit(solution)/shard_map/reduce_scatter | solution.py:60
  27.2 63.9 %copy-start.9 = (f32[256,1024]{1,0:T(8,128)S(1)}, f32[256,1024]{1,0:T(8,128)}, u32[]{:S(2)}) copy-start(f32[256,1024]{1,0:T(8,128)} %param.9) | copy-start | bytes 3145732
  27.2 63.9 %copy-start.10 = (f32[8,128,128]{2,1,0:T(8,128)S(1)}, f32[8,128,128]{2,1,0:T(8,128)}, u32[]{:S(2)}) copy-start(f32[8,128,128]{2,1,0:T(8,128)} %param.12) | copy-start | bytes 1572868
  94.4 1.5 copy-start.4
  94.6 1.0 copy-start.1
  260.6 2.5 copy-start.2
  263.1 2.0 copy-start.5
  263.1 2.0 copy-start.7
  387.6 90.0 %copy-start.8 = (f32[256,1024]{1,0:T(8,128)S(1)}, f32[256,1024]{1,0:T(8,128)}, u32[]{:S(2)}) copy-start(f32[256,1024]{1,0:T(8,128)} %param.15) | copy-start | bytes 3145732
Sparse Core Ops, SparseCore 0:
  16.7 241.3 all-gather.6
  260.9 96.2 all-gather.4
  387.7 89.7 reduce-scatter.1
where the time goes:
time: 492 us; the launch traced here: 486 us
  waiting for transfers between devices  337 us (68%)
  blocking collectives  71.4 us (15%)
  matrix products  48.2 us (10%)
  between operations  13.3 us (3%)
  other arithmetic  9.65 us (2%)
  local copies, waits for them, and re-layouts  6.49 us (1%)
    all_gather x1, waiting for transfers between devices, carried_in(): gathered = jax.tree.map(lambda a: lax.all_gather(a, axis), part)  157 us
    reduce_scatter x1, waiting for transfers between devices, body(): lax.psum_scatter(partial_value, 'head', scatter_dimension=1, tiled=True)  89.9 us
    all_gather x1, waiting for transfers between devices, body(): lax.all_gather(own_rows, 'ctx', axis=1, tiled=True)  89.8 us
    all_gather x1, blocking collectives, carried_in(): gathered = jax.tree.map(lambda a: lax.all_gather(a, axis), part)  60.9 us
    dot_general x1, matrix products, body(): jnp.dot(mixed, lax.all_gather(own_rows, 'ctx', axis=1, tiled=True), preci...  30.4 us
    all_to_all x1, blocking collectives, body(): lax.all_to_all(out_weight, 'head', split_axis=0, concat_axis=1, tiled=True)  10.4 us
  transfers between devices with their start and end apart: 3, of which 3 were waited for; matrix products, arithmetic and copies ran while one was open for 4% of the time, Pallas kernels for 0%

commit v1 on v0

v1 whole, which is shorter than its diff:
```python
import jax
import jax.numpy as jnp
from jax import lax
from jax.experimental import pallas as pl
from jax.experimental.pallas import tpu as pltpu
from jax.sharding import PartitionSpec as P

MESH = pl.DeviceIdType.MESH
NX, NY, NZ = 4, 4, 8
ROWS, HEADS, HD, FEAT = 256, 8, 128, 256
WIDTH = HEADS * HD
HALF = 2048
KX = 1280
KZ = HALF - KX
SUBS = ((0, 72), (72, 64))
SROWS = 136
CHUNKS = 2
CR = ROWS // CHUNKS
F32, BF16 = jnp.float32, jnp.bfloat16

NN = (((1,), (0,)), ((), ()))
NT = (((1,), (1,)), ((), ()))


def split(a):
    high = a.astype(BF16)
    return high, (a - high.astype(F32)).astype(BF16)


def dot3(a, b, dims):
    (ah, al), (bh, bl) = a, b

    def one(p, q):
        return lax.dot_general(p, q, dims, preferred_element_type=F32)

    return one(ah, bh) + (one(ah, bl) + one(al, bh))


def features(inputs, weights):
    s = dot3(split(inputs), split(weights), NN)
    up = jnp.exp(s - jnp.max(s, axis=1, keepdims=True))
    down = jnp.exp(jnp.min(s, axis=1, keepdims=True) - s)
    up = up / jnp.sum(up, axis=1, keepdims=True)
    down = down / jnp.sum(down, axis=1, keepdims=True)
    return jnp.concatenate([up, down], axis=1)


def kernel(
    q_ref, k_ref, v_ref, qm_ref, km_ref, wt_ref, out_ref,
    qfh, qfl, kfh, kfl, nl, dl, st, rr, bk, pf, zp, zs,
    wb, wh, wl, ab, ah, al, co, cs, cr, fr,
    yg_s, yg_r, xa_s, xa_r, zx_s, zx_r, zz_s, zz_r, xz_s, xz_r,
    aa_s, aa_r, ch_s, ch_r, bb_s, bb_r, m_s, m_r, c_s, c_r, f_s, f_r,
):
    ctx, y = lax.axis_index("ctx"), lax.axis_index("head")
    core, r = lax.rem(ctx, 2), lax.rem(ctx, 8)
    x, z = lax.div(r, 2), lax.div(ctx, 8)
    row0 = ctx - r
    yp = lax.rem(y, 2)
    pair = y + 1 - 2 * yp
    far = 3 - y
    other = ctx + 1 - 2 * core
    pending = []

    def at(zz, xx):
        return ((zz * NX + xx) * 2 + core, y)

    def copy(src, dst, send, recv, device):
        return pltpu.make_async_remote_copy(
            src_ref=src, dst_ref=dst, send_sem=send, recv_sem=recv, device_id=device, device_id_type=MESH
        )

    def send(src, dst, ss, rs, device, when=None):
        c = copy(src, dst, ss, rs, device)
        if when is None:
            c.start()
        else:
            pl.when(when)(c.start)
        pending.append((when, c))

    def recv(dst, rs, when=None):
        c = copy(dst, dst, rs, rs, (ctx, y))
        if when is None:
            c.wait_recv()
        else:
            pl.when(when)(c.wait_recv)

    def member(zz):
        a = jnp.where(lax.rem(zz + 2, NZ) < 4, 0, 1)
        return jnp.logical_or(y == a, y == 3 - a)

    def slot(zz):
        return lax.rem(zz, 2) + jnp.where(lax.div(zz, 2) == y, 0, 2)

    barrier = pltpu.get_barrier_semaphore()
    greeted = [(ctx, lax.rem(y + i, NY)) for i in range(1, NY)]
    greeted += [(row0 + lax.rem(r + i, 8), y) for i in range(1, 8)]
    greeted += [at(lax.rem(z + 1, NZ), x), at(lax.rem(z + NZ - 1, NZ), x)]
    for device in greeted:
        pl.semaphore_signal(barrier, inc=1, device_id=device, device_id_type=MESH)
    pl.semaphore_wait(barrier, len(greeted))

    mine = member(z)
    my_slot = slot(z)
    first = jnp.where(lax.rem(z + 2, NZ) < 4, 0, 1)
    my_rows = pl.ds(pl.multiple_of(16 * y, 16), 16)
    for part in range(2):
        to = first if part == 0 else 3 - first
        there = lax.rem(z, 2) + jnp.where(lax.div(z, 2) == to, 0, 2)
        src = wt_ref.at[:, pl.ds(part * HALF, HALF)]
        send(src, wb.at[there, x, my_rows, :], yg_s.at[part], yg_r.at[y], (ctx, to), to != y)

        @pl.when(to == y)
        def _(there=there, part=part):
            wb[there, x, my_rows, :] = wt_ref[:, part * HALF : (part + 1) * HALF]

    def weights_y_done():
        for i in range(1, NY):
            yy = lax.rem(y + i, NY)
            recv(wb.at[my_slot, x, pl.ds(pl.multiple_of(16 * yy, 16), 16), :], yg_r.at[yy], mine)

    def weights_x_send():
        for i in range(1, NX):
            xx = lax.rem(x + i, NX)
            block = wb.at[my_slot, x, :, pl.ds(KZ, KX)]
            send(block, block, xa_s.at[i - 1], xa_r.at[x], at(z, xx), mine)

    def weights_x_done():
        for i in range(1, NX):
            xx = lax.rem(x + i, NX)
            recv(wb.at[my_slot, xx, :, pl.ds(KZ, KX)], xa_r.at[xx], mine)

    def ring(zz, d, n):
        return lax.rem(zz + (n if d == 0 else NZ - n) + NZ, NZ)

    def ring_x(d, s, i):
        xx = lax.rem(x + i, NX)
        source = ring(z, 1 - d, s)
        block = wb.at[slot(source), xx, :, pl.ds(KZ + d * (KX // 2), KX // 2)]
        have = member(source)
        if s > 0:
            recv(block, zx_r.at[d, s - 1, xx], have)
        if s < NZ - 1:
            send(block, block, zx_s.at[d, s, xx], zx_r.at[d, s, xx], at(ring(z, d, 1), x), have)

    def ring_z(d, s):
        source = ring(z, 1 - d, s)
        block = wb.at[slot(source), x, :, pl.ds(d * (KZ // 2), KZ // 2)]
        have = member(source)
        if s > 0:
            recv(block, zz_r.at[d, s - 1], have)
        if s < NZ - 1:
            send(block, block, zz_s.at[d, s], zz_r.at[d, s], at(ring(z, d, 1), x), have)
        for i in range(1, NX):
            xx = lax.rem(x + i, NX)
            send(block, block, xz_s.at[d, s, i - 1], xz_r.at[d, s, x], at(z, xx), have)

    def ring_z_done(d, s):
        source = ring(z, 1 - d, s)
        for i in range(1, NX):
            xx = lax.rem(x + i, NX)
            recv(wb.at[slot(source), xx, :, pl.ds(d * (KZ // 2), KZ // 2)], xz_r.at[d, s, xx], member(source))

    def weights_split():
        def one(i, carry):
            zi, xx = lax.div(i, NX), lax.rem(i, NX)
            high, low = split(wb[zi, xx])
            rows = pl.ds(pl.multiple_of(i * 64, 64), 64)
            wh[rows, :] = high
            wl[rows, :] = low
            return carry

        lax.fori_loop(0, 16, one, 0)

    def keys(h):
        cols = slice(h * HD, (h + 1) * HD)
        kf = features(k_ref[:, cols], km_ref[h])
        high, low = split(kf)
        kfh[h] = high
        kfl[h] = low
        st[h, 0:HD, :] = dot3(split(v_ref[:, cols].T), (high, low), NN)
        st[h, HD:SROWS, :] = jnp.broadcast_to(jnp.sum(kf, axis=0, keepdims=True), (SROWS - HD, FEAT))
        for n, (start, size) in enumerate(SUBS):
            rows = pl.ds(start, size)
            send(st.at[h, rows, :], rr.at[r, rows, :], aa_s.at[h, n], aa_r.at[r, n], (row0 + h, y), r != h)

        @pl.when(r == h)
        def _():
            rr[h] = st[h]

    def queries(h):
        cols = slice(h * HD, (h + 1) * HD)
        qf = split(features(q_ref[:, cols], qm_ref[h]))
        qfh[h], qfl[h] = qf
        w = dot3(qf, (kfh[h], kfl[h]), NT)
        causal = lax.broadcasted_iota(jnp.int32, (ROWS, ROWS), 0) >= lax.broadcasted_iota(jnp.int32, (ROWS, ROWS), 1)
        w = jnp.where(causal, w, 0.0)
        dl[h] = jnp.broadcast_to(jnp.sum(w, axis=1, keepdims=True), (ROWS, HD))
        nl[h] = dot3(split(w), split(v_ref[:, cols]), NN)

    def row_sums(n):
        start, size = SUBS[n]
        rows = pl.ds(start, size)
        for i in range(1, 8):
            j = lax.rem(r + i, 8)
            recv(rr.at[j, rows, :], aa_r.at[j, n])
        total = jnp.zeros((size, FEAT), F32)
        for i in range(8):
            bk[i, start : start + size, :] = total
            total = total + rr[i, start : start + size, :]
        zs[start : start + size, :] = total

    def chain(n):
        start, size = SUBS[n]
        rows = pl.ds(start, size)
        recv(zp.at[rows, :], ch_r.at[n], z > 0)

        @pl.when(z == 0)
        def _():
            zp[start : start + size, :] = jnp.zeros((size, FEAT), F32)

        @pl.when(z > 0)
        def _():
            zs[start : start + size, :] += zp[start : start + size, :]

        send(zs.at[rows, :], zp.at[rows, :], ch_s.at[n], ch_r.at[n], at(lax.rem(z + 1, NZ), x), z < NZ - 1)

    def send_back(n):
        start, size = SUBS[n]
        rows = pl.ds(start, size)
        before = zp[start : start + size, :]
        for i in range(8):
            bk[i, start : start + size, :] += before
            send(bk.at[i, rows, :], pf.at[r, rows, :], bb_s.at[i, n], bb_r.at[r, n], (row0 + i, y), r != i)

            @pl.when(r == i)
            def _(i=i):
                pf[i, start : start + size, :] = bk[i, start : start + size, :]

    def prefix_done():
        for n, (start, size) in enumerate(SUBS):
            for i in range(1, 8):
                j = lax.rem(r + i, 8)
                recv(pf.at[j, pl.ds(start, size), :], bb_r.at[j, n])

    def mix(c):
        rows = pl.ds(c * CR, CR)
        for h in range(HEADS):
            state = pf[h]
            qf = (qfh[h, c * CR : (c + 1) * CR, :], qfl[h, c * CR : (c + 1) * CR, :])
            far_sum = dot3(qf, split(state), NT)
            denom = dl[h, c * CR : (c + 1) * CR, :] + far_sum[:, HD : HD + 1]
            ab[yp, core, rows, h * HD : (h + 1) * HD] = (nl[h, c * CR : (c + 1) * CR, :] + far_sum[:, :HD]) / denom
        block = ab.at[yp, core, rows, :]
        send(block, block, m_s.at[c, 0], m_r.at[c, 0], (ctx, pair))
        send(block, block, m_s.at[c, 1], m_r.at[c, 1], (other, y))

    def relay(c):
        rows = pl.ds(c * CR, CR)
        block = ab.at[1 - yp, core, rows, :]
        recv(block, m_r.at[c, 0])
        send(block, block, m_s.at[c, 2], m_r.at[c, 2], (other, y))

    def project(c):
        rows = pl.ds(c * CR, CR)
        recv(ab.at[yp, 1 - core, rows, :], m_r.at[c, 1])
        recv(ab.at[1 - yp, 1 - core, rows, :], m_r.at[c, 2])
        for cc in range(2):
            for yy in range(2):
                high, low = split(ab[yy, cc, c * CR : (c + 1) * CR, :])
                ah[cc * CR : (cc + 1) * CR, yy * WIDTH : (yy + 1) * WIDTH] = high
                al[cc * CR : (cc + 1) * CR, yy * WIDTH : (yy + 1) * WIDTH] = low
        for base, dst in ((512, cs), (0, co)):

            def one(n, carry, base=base, dst=dst):
                wrows = pl.ds(pl.multiple_of(base + n * 256, 256), 256)
                cols = pl.ds(pl.multiple_of(n * 256, 256), 256)
                dst[c, :, cols] = dot3((ah[...], al[...]), (wh[wrows, :], wl[wrows, :]), NT)
                return carry

            lax.fori_loop(0, 2, one, 0)
            if base:
                send(cs.at[c], cr.at[c], c_s.at[c], c_r.at[c], (ctx, far))

    def gather(c):
        recv(cr.at[c], c_r.at[c])
        co[c] += cr[c]
        theirs = co.at[c, pl.ds(pl.multiple_of((1 - core) * CR, CR), CR), :]
        send(theirs, fr.at[c], f_s.at[c], f_r.at[c], (other, y))

    def finish(c):
        recv(fr.at[c], f_r.at[c])
        low_half = lax.broadcasted_iota(jnp.int32, (CR, 128), 1) < 64
        for cc in range(2):

            @pl.when(core == cc)
            def _(cc=cc):
                for m in range(4):
                    cols = slice(m * 128, (m + 1) * 128)
                    a, b = co[c, cc * CR : (cc + 1) * CR, cols], fr[c, :, cols]
                    if cc:
                        a, b = b, a
                    out_ref[c * CR : (c + 1) * CR, m * 256 : m * 256 + 128] = jnp.where(low_half, a, pltpu.roll(b, 64, 1))
                    out_ref[c * CR : (c + 1) * CR, m * 256 + 128 : (m + 1) * 256] = jnp.where(
                        low_half, pltpu.roll(a, 64, 1), b
                    )

    def ring_step(s):
        for i in range(NX):
            for d in range(2):
                ring_x(d, s, i)
        for d in range(2):
            ring_z(d, s)

    for h in range(HEADS):
        keys(h)
        if h == 3:
            weights_y_done()
            weights_x_send()
            for d in range(2):
                ring_z(d, 0)
    weights_x_done()
    for i in range(NX):
        for d in range(2):
            ring_x(d, 0, i)
    for h in range(HEADS):
        queries(h)
        if h == 4:
            for n in range(len(SUBS)):
                row_sums(n)
    ring_step(1)
    for n in range(len(SUBS)):
        chain(n)
    for n in range(len(SUBS)):
        send_back(n)
    for s in range(2, NZ):
        ring_step(s)
    prefix_done()
    for c in range(CHUNKS):
        mix(c)
    for s in range(NZ):
        for d in range(2):
            ring_z_done(d, s)
    weights_split()
    relay(0)
    for c in range(CHUNKS):
        project(c)
        if c + 1 < CHUNKS:
            relay(c + 1)
        if c > 0:
            gather(c - 1)
    gather(CHUNKS - 1)
    for c in range(CHUNKS):
        finish(c)
    for when, c in pending:
        if when is None:
            c.wait_send()
        else:
            pl.when(when)(c.wait_send)


def attend(q, k, v, qm, km, wt):
    dma = pltpu.SemaphoreType.DMA
    subs = len(SUBS)
    vmem = pltpu.VMEM
    scratch = [
        vmem((HEADS, ROWS, FEAT), BF16), vmem((HEADS, ROWS, FEAT), BF16),
        vmem((HEADS, ROWS, FEAT), BF16), vmem((HEADS, ROWS, FEAT), BF16),
        vmem((HEADS, ROWS, HD), F32), vmem((HEADS, ROWS, HD), F32),
        vmem((HEADS, SROWS, FEAT), F32), vmem((HEADS, SROWS, FEAT), F32),
        vmem((HEADS, SROWS, FEAT), F32), vmem((HEADS, SROWS, FEAT), F32),
        vmem((SROWS, FEAT), F32), vmem((SROWS, FEAT), F32),
        vmem((4, NX, 64, HALF), F32), vmem((1024, HALF), BF16), vmem((1024, HALF), BF16),
        vmem((2, 2, ROWS, WIDTH), F32), vmem((2 * CR, HALF), BF16), vmem((2 * CR, HALF), BF16),
        vmem((CHUNKS, 2 * CR, 512), F32), vmem((CHUNKS, 2 * CR, 512), F32),
        vmem((CHUNKS, 2 * CR, 512), F32), vmem((CHUNKS, CR, 512), F32),
        dma((2,)), dma((NY,)), dma((3,)), dma((NX,)),
        dma((2, NZ - 1, NX)), dma((2, NZ - 1, NX)), dma((2, NZ - 1)), dma((2, NZ - 1)),
        dma((2, NZ, 3)), dma((2, NZ, NX)),
        dma((8, subs)), dma((8, subs)), dma((subs,)), dma((subs,)), dma((8, subs)), dma((8, subs)),
        dma((CHUNKS, 3)), dma((CHUNKS, 3)), dma((CHUNKS,)), dma((CHUNKS,)), dma((CHUNKS,)), dma((CHUNKS,)),
    ]
    return pl.pallas_call(
        kernel,
        out_shape=jax.ShapeDtypeStruct((ROWS, WIDTH), F32),
        in_specs=[pl.BlockSpec(memory_space=vmem)] * 6,
        out_specs=pl.BlockSpec(memory_space=vmem),
        scratch_shapes=scratch,
        compiler_params=pltpu.CompilerParams(
            collective_id=0, has_side_effects=True, vmem_limit_bytes=60 * 1024 * 1024
        ),
    )(q, k, v, qm, km, wt)


def body(queries, keys, values, query_map, key_map, out_weight, residual):
    return residual + attend(queries, keys, values, query_map, key_map, out_weight.T)


def solution(mesh):
    placed = (
        P("ctx", "head"),
        P("ctx", "head"),
        P("ctx", "head"),
        P("head", None, None),
        P("head", None, None),
        P(None, ("ctx", "head")),
        P("ctx", "head"),
    )
    return jax.shard_map(body, mesh=mesh, in_specs=placed, out_specs=P("ctx", "head"), check_vma=False)
```

time: 492 us -> 207 us (0.42)
  the two profiles are of different devices: /device:TPU:1 before, /device:TPU:79 now
where the time goes in v1:
time: 207 us; the launch traced here: 206 us
  Pallas kernels  204 us (99%)
  other arithmetic  2.38 us (1%)
    pallas_call x1, Pallas kernels, attend(): pl.pallas_call(kernel, out_shape=jax.ShapeDtypeStruct((ROWS, WIDTH), F32)...  204 us

profile of v1, /device:TPU:79, one launch (start us, length us, event | category | flops | bytes accessed | tf_op | source)
XLA Modules:
  0.0 206.5 jit_solution(9501949893018579215)
XLA Ops:
  0.0 0.0 copy-start
  0.0 204.1 %shard_map.73 = f32[256,1024]{1,0:T(8,128)} custom-call(f32[256,1024]{1,0:T(8,128)} %q_ref.1, f32[256,1024]{1,0:T(8,128)} %k_ref.1, f32[256,1024]{1,0:T(8,128)} %v_ref.1, f32[8,128,128]{2,1,0:T(8,128)} %qm_ref.1, f32[8,128,128]{2,1,0:T(8,128)} %km_ref.1, f32[16,4096]{1,0:T(8,128)} %bitcast.1), custom_call_target="tpu_custom_call" | custom-call | tf_op jit(solution)/shard_map/pallas_call | solution.py:383
  204.1 0.0 copy-done
  204.1 2.4 %add.3 = f32[256,1024]{1,0:T(8,128)} add(f32[256,1024]{1,0:T(8,128)S(1)} %copy-done, f32[256,1024]{1,0:T(8,128)} %shard_map.73) | non-fusion elementwise | flops 262144 | bytes 3145728 | tf_op jit(solution)/shard_map/add | solution.py:396
Async XLA Ops:
  0.0 204.1 %copy-start = (f32[256,1024]{1,0:T(8,128)S(1)}, f32[256,1024]{1,0:T(8,128)}, u32[]{:S(2)}) copy-start(f32[256,1024]{1,0:T(8,128)} %param.13) | copy-start | bytes 3145732

commit v2 on v1

--- a/solution.py
+++ b/solution.py
@@ -10,8 +10,10 @@
 ROWS, HEADS, HD, FEAT = 256, 8, 128, 256
 WIDTH = HEADS * HD
 HALF = 2048
-KX = 1280
-KZ = HALF - KX
+KP = 1024
+KZ = 384
+KX = KP - KZ
+ZHALF = ((0, 256), (256, 128))
 SUBS = ((0, 72), (72, 64))
 SROWS = 136
 CHUNKS = 2
@@ -92,74 +94,92 @@
     def slot(zz):
         return lax.rem(zz, 2) + jnp.where(lax.div(zz, 2) == y, 0, 2)
 
+    def twin(zz):
+        return zz + 2 - 4 * lax.rem(lax.div(zz, 2), 2)
+
     barrier = pltpu.get_barrier_semaphore()
     greeted = [(ctx, lax.rem(y + i, NY)) for i in range(1, NY)]
     greeted += [(row0 + lax.rem(r + i, 8), y) for i in range(1, 8)]
     greeted += [at(lax.rem(z + 1, NZ), x), at(lax.rem(z + NZ - 1, NZ), x)]
+    greeted += [(at(twin(z), x)[0], lax.rem(y + i, NY)) for i in range(NY)]
     for device in greeted:
         pl.semaphore_signal(barrier, inc=1, device_id=device, device_id_type=MESH)
     pl.semaphore_wait(barrier, len(greeted))
 
-    mine = member(z)
-    my_slot = slot(z)
     first = jnp.where(lax.rem(z + 2, NZ) < 4, 0, 1)
     my_rows = pl.ds(pl.multiple_of(16 * y, 16), 16)
     for part in range(2):
         to = first if part == 0 else 3 - first
         there = lax.rem(z, 2) + jnp.where(lax.div(z, 2) == to, 0, 2)
-        src = wt_ref.at[:, pl.ds(part * HALF, HALF)]
-        send(src, wb.at[there, x, my_rows, :], yg_s.at[part], yg_r.at[y], (ctx, to), to != y)
+        low = slice(part * HALF, part * HALF + KP)
+        dst = wb.at[there, x, my_rows, pl.ds(KP, KP)]
+        send(wt_ref.at[:, pl.ds(part * HALF + KP, KP)], dst, yg_s.at[part, 1], yg_r.at[y], (at(twin(z), x)[0], to))
+        dst = wb.at[there, x, my_rows, pl.ds(0, KP)]
+        send(wt_ref.at[:, pl.ds(part * HALF, KP)], dst, yg_s.at[part, 0], yg_r.at[y], (ctx, to), to != y)
 
         @pl.when(to == y)
-        def _(there=there, part=part):
-            wb[there, x, my_rows, :] = wt_ref[:, part * HALF : (part + 1) * HALF]
+        def _(there=there, low=low):
+            wb[there, x, my_rows, 0:KP] = wt_ref[:, low]
+
+    def block_of(zz, xx, start, size):
+        has = member(zz)
+        at_slot = slot(jnp.where(has, zz, twin(zz)))
+        cols = pl.ds(pl.multiple_of(jnp.where(has, start, KP + start), 128), size)
+        return wb.at[at_slot, xx, :, cols]
 
     def weights_y_done():
-        for i in range(1, NY):
+        has = member(z)
+        at_slot = slot(jnp.where(has, z, twin(z)))
+        cols = pl.ds(pl.multiple_of(jnp.where(has, 0, KP), 128), KP)
+        for i in range(NY):
             yy = lax.rem(y + i, NY)
-            recv(wb.at[my_slot, x, pl.ds(pl.multiple_of(16 * yy, 16), 16), :], yg_r.at[yy], mine)
+            rows = pl.ds(pl.multiple_of(16 * yy, 16), 16)
+            recv(wb.at[at_slot, x, rows, cols], yg_r.at[yy], jnp.logical_not(has) if i == 0 else None)
 
     def weights_x_send():
         for i in range(1, NX):
             xx = lax.rem(x + i, NX)
-            block = wb.at[my_slot, x, :, pl.ds(KZ, KX)]
-            send(block, block, xa_s.at[i - 1], xa_r.at[x], at(z, xx), mine)
-
-    def weights_x_done():
-        for i in range(1, NX):
-            xx = lax.rem(x + i, NX)
-            recv(wb.at[my_slot, xx, :, pl.ds(KZ, KX)], xa_r.at[xx], mine)
+            block = block_of(z, x, KZ, KX)
+            send(block, block, xa_s.at[i - 1], xa_r.at[x], at(z, xx))
+
+    def weights_x_done(i):
+        xx = lax.rem(x + i, NX)
+        recv(block_of(z, xx, KZ, KX), xa_r.at[xx])
 
     def ring(zz, d, n):
-        return lax.rem(zz + (n if d == 0 else NZ - n) + NZ, NZ)
+        return lax.rem(zz + (n if d == 0 else NZ - n), NZ)
 
     def ring_x(d, s, i):
         xx = lax.rem(x + i, NX)
-        source = ring(z, 1 - d, s)
-        block = wb.at[slot(source), xx, :, pl.ds(KZ + d * (KX // 2), KX // 2)]
-        have = member(source)
-        if s > 0:
-            recv(block, zx_r.at[d, s - 1, xx], have)
-        if s < NZ - 1:
-            send(block, block, zx_s.at[d, s, xx], zx_r.at[d, s, xx], at(ring(z, d, 1), x), have)
+        block = block_of(ring(z, 1 - d, s), xx, KZ, KX)
+        last = i // 2 == d
+        if s > 0 and (s < 4 or last):
+            recv(block, zx_r.at[d, s - 1, xx])
+        if s < 3 or (s == 3 and last):
+            send(block, block, zx_s.at[d, s, xx], zx_r.at[d, s, xx], at(ring(z, d, 1), x))
 
     def ring_z(d, s):
         source = ring(z, 1 - d, s)
-        block = wb.at[slot(source), x, :, pl.ds(d * (KZ // 2), KZ // 2)]
-        have = member(source)
+        start, size = ZHALF[d] if s == 4 else (0, KZ)
+        block = block_of(source, x, start, size)
         if s > 0:
-            recv(block, zz_r.at[d, s - 1], have)
-        if s < NZ - 1:
-            send(block, block, zz_s.at[d, s], zz_r.at[d, s], at(ring(z, d, 1), x), have)
-        for i in range(1, NX):
-            xx = lax.rem(x + i, NX)
-            send(block, block, xz_s.at[d, s, i - 1], xz_r.at[d, s, x], at(z, xx), have)
+            recv(block, zz_r.at[d, s - 1])
+        if s < 4:
+            start, size = ZHALF[d] if s == 3 else (0, KZ)
+            part = block_of(source, x, start, size)
+            send(part, part, zz_s.at[d, s], zz_r.at[d, s], at(ring(z, d, 1), x))
+        if s > 0 or d == 0:
+            for i in range(1, NX):
+                xx = lax.rem(x + i, NX)
+                send(block, block, xz_s.at[d, s, i - 1], xz_r.at[d, s, x], at(z, xx))
 
     def ring_z_done(d, s):
         source = ring(z, 1 - d, s)
-        for i in range(1, NX):
-            xx = lax.rem(x + i, NX)
-            recv(wb.at[slot(source), xx, :, pl.ds(d * (KZ // 2), KZ // 2)], xz_r.at[d, s, xx], member(source))
+        start, size = ZHALF[d] if s == 4 else (0, KZ)
+        if s > 0 or d == 0:
+            for i in range(1, NX):
+                xx = lax.rem(x + i, NX)
+                recv(block_of(source, xx, start, size), xz_r.at[d, s, xx])
 
     def weights_split():
         def one(i, carry):
@@ -309,36 +329,41 @@
         for i in range(NX):
             for d in range(2):
                 ring_x(d, s, i)
-        for d in range(2):
-            ring_z(d, s)
+            if i == 0:
+                for d in range(2):
+                    ring_z(d, s)
 
     for h in range(HEADS):
         keys(h)
-        if h == 3:
+        if h == 1:
             weights_y_done()
             weights_x_send()
             for d in range(2):
+                ring_x(d, 0, 0)
                 ring_z(d, 0)
-    weights_x_done()
-    for i in range(NX):
-        for d in range(2):
-            ring_x(d, 0, i)
+        if h == 4:
+            for i in range(1, NX):
+                weights_x_done(i)
+                for d in range(2):
+                    ring_x(d, 0, i)
     for h in range(HEADS):
         queries(h)
+        if h == 1:
+            ring_step(1)
         if h == 4:
             for n in range(len(SUBS)):
                 row_sums(n)
-    ring_step(1)
     for n in range(len(SUBS)):
         chain(n)
+    ring_step(2)
     for n in range(len(SUBS)):
         send_back(n)
-    for s in range(2, NZ):
-        ring_step(s)
+    ring_step(3)
+    ring_step(4)
     prefix_done()
     for c in range(CHUNKS):
         mix(c)
-    for s in range(NZ):
+    for s in range(5):
         for d in range(2):
             ring_z_done(d, s)
     weights_split()
@@ -374,9 +399,9 @@
         vmem((2, 2, ROWS, WIDTH), F32), vmem((2 * CR, HALF), BF16), vmem((2 * CR, HALF), BF16),
         vmem((CHUNKS, 2 * CR, 512), F32), vmem((CHUNKS, 2 * CR, 512), F32),
         vmem((CHUNKS, 2 * CR, 512), F32), vmem((CHUNKS, CR, 512), F32),
-        dma((2,)), dma((NY,)), dma((3,)), dma((NX,)),
-        dma((2, NZ - 1, NX)), dma((2, NZ - 1, NX)), dma((2, NZ - 1)), dma((2, NZ - 1)),
-        dma((2, NZ, 3)), dma((2, NZ, NX)),
+        dma((2, 2)), dma((NY,)), dma((3,)), dma((NX,)),
+        dma((2, 4, NX)), dma((2, 4, NX)), dma((2, 4)), dma((2, 4)),
+        dma((2, 5, 3)), dma((2, 5, NX)),
         dma((8, subs)), dma((8, subs)), dma((subs,)), dma((subs,)), dma((8, subs)), dma((8, subs)),
         dma((CHUNKS, 3)), dma((CHUNKS, 3)), dma((CHUNKS,)), dma((CHUNKS,)), dma((CHUNKS,)), dma((CHUNKS,)),
     ]

time: 207 us -> 148 us (0.71)
  the two profiles are of different devices: /device:TPU:79 before, /device:TPU:1 now
where the time goes in v2:
time: 148 us; the launch traced here: 145 us
  Pallas kernels  143 us (97%)
  other arithmetic  2.38 us (2%)
    pallas_call x1, Pallas kernels, attend(): pl.pallas_call(kernel, out_shape=jax.ShapeDtypeStruct((ROWS, WIDTH), F32)...  143 us

profile of v2, /device:TPU:1, one launch (start us, length us, event | category | flops | bytes accessed | tf_op | source)
XLA Modules:
  0.0 145.2 jit_solution(11256441604340591788)
XLA Ops:
  0.0 0.0 copy-start
  0.0 142.8 %shard_map.73 = f32[256,1024]{1,0:T(8,128)} custom-call(f32[256,1024]{1,0:T(8,128)} %q_ref.1, f32[256,1024]{1,0:T(8,128)} %k_ref.1, f32[256,1024]{1,0:T(8,128)} %v_ref.1, f32[8,128,128]{2,1,0:T(8,128)} %qm_ref.1, f32[8,128,128]{2,1,0:T(8,128)} %km_ref.1, f32[16,4096]{1,0:T(8,128)} %bitcast.1), custom_call_target="tpu_custom_call" | custom-call | tf_op jit(solution)/shard_map/pallas_call | solution.py:408
  142.8 0.0 copy-done
  142.9 2.4 %add.3 = f32[256,1024]{1,0:T(8,128)} add(f32[256,1024]{1,0:T(8,128)S(1)} %copy-done, f32[256,1024]{1,0:T(8,128)} %shard_map.73) | non-fusion elementwise | flops 262144 | bytes 3145728 | tf_op jit(solution)/shard_map/add | solution.py:421
Async XLA Ops:
  0.0 142.8 %copy-start = (f32[256,1024]{1,0:T(8,128)S(1)}, f32[256,1024]{1,0:T(8,128)}, u32[]{:S(2)}) copy-start(f32[256,1024]{1,0:T(8,128)} %param.13) | copy-start | bytes 3145732

commit v3 on v2

--- a/solution.py
+++ b/solution.py
@@ -11,12 +11,12 @@
 WIDTH = HEADS * HD
 HALF = 2048
 KP = 1024
-KZ = 384
+KZ = 512
 KX = KP - KZ
-ZHALF = ((0, 256), (256, 128))
-SUBS = ((0, 72), (72, 64))
+ZHALF = ((0, 256), (256, 256))
+PIECE = 16
 SROWS = 136
-CHUNKS = 2
+CHUNKS = 4
 CR = ROWS // CHUNKS
 F32, BF16 = jnp.float32, jnp.bfloat16
 
@@ -49,15 +49,14 @@
 
 def kernel(
     q_ref, k_ref, v_ref, qm_ref, km_ref, wt_ref, out_ref,
-    qfh, qfl, kfh, kfl, nl, dl, st, rr, bk, pf, zp, zs,
+    qfh, qfl, kfh, kfl, nl, dl, st, sp, su, rr, bk, pc, sd, pf, zt, zr, zb, zp,
     wb, wh, wl, ab, ah, al, co, cs, cr, fr,
     yg_s, yg_r, xa_s, xa_r, zx_s, zx_r, zz_s, zz_r, xz_s, xz_r,
-    aa_s, aa_r, ch_s, ch_r, bb_s, bb_r, m_s, m_r, c_s, c_r, f_s, f_r,
+    dd_s, dd_r, aa_s, aa_r, z1_s, z1_r, z2_s, z2_r, bb_s, bb_r, ee_s, ee_r, m_s, m_r, c_s, c_r, f_s, f_r,
 ):
     ctx, y = lax.axis_index("ctx"), lax.axis_index("head")
     core, r = lax.rem(ctx, 2), lax.rem(ctx, 8)
     x, z = lax.div(r, 2), lax.div(ctx, 8)
-    row0 = ctx - r
     yp = lax.rem(y, 2)
     pair = y + 1 - 2 * yp
     far = 3 - y
@@ -99,9 +98,9 @@
 
     barrier = pltpu.get_barrier_semaphore()
     greeted = [(ctx, lax.rem(y + i, NY)) for i in range(1, NY)]
-    greeted += [(row0 + lax.rem(r + i, 8), y) for i in range(1, 8)]
-    greeted += [at(lax.rem(z + 1, NZ), x), at(lax.rem(z + NZ - 1, NZ), x)]
-    greeted += [(at(twin(z), x)[0], lax.rem(y + i, NY)) for i in range(NY)]
+    greeted += [at(z, lax.rem(x + i, NX)) for i in range(1, NX)] + [(other, y)]
+    greeted += [at(lax.rem(z + i, NZ), x) for i in range(1, NZ)]
+    greeted += [(at(twin(z), x)[0], lax.rem(y + i, NY)) for i in range(1, NY)]
     for device in greeted:
         pl.semaphore_signal(barrier, inc=1, device_id=device, device_id_type=MESH)
     pl.semaphore_wait(barrier, len(greeted))
@@ -169,17 +168,29 @@
             part = block_of(source, x, start, size)
             send(part, part, zz_s.at[d, s], zz_r.at[d, s], at(ring(z, d, 1), x))
         if s > 0 or d == 0:
-            for i in range(1, NX):
-                xx = lax.rem(x + i, NX)
-                send(block, block, xz_s.at[d, s, i - 1], xz_r.at[d, s, x], at(z, xx))
-
-    def ring_z_done(d, s):
+            for k in range(2):
+                send(block, block, xz_s.at[d, s, k], xz_r.at[d, s, k], at(z, beside(k)))
+
+    def beside(k, n=1):
+        return lax.rem(x + (n if k == 0 else NX - n), NX)
+
+    def relay_z(d, s):
+        if s == 0 and d == 1:
+            return
         source = ring(z, 1 - d, s)
         start, size = ZHALF[d] if s == 4 else (0, KZ)
-        if s > 0 or d == 0:
-            for i in range(1, NX):
-                xx = lax.rem(x + i, NX)
-                recv(block_of(source, xx, start, size), xz_r.at[d, s, xx])
+        for k in range(2):
+            recv(block_of(source, beside(1 - k), start, size), xz_r.at[d, s, k])
+            half = block_of(source, beside(1 - k), start + k * (size // 2), size // 2)
+            send(half, half, xz_s.at[d, s, 2 + k], xz_r.at[d, s, 2 + k], at(z, beside(k)))
+
+    def ring_z_done(d, s):
+        if s == 0 and d == 1:
+            return
+        source = ring(z, 1 - d, s)
+        start, size = ZHALF[d] if s == 4 else (0, KZ)
+        for k in range(2):
+            recv(block_of(source, beside(1 - k, 2), start + k * (size // 2), size // 2), xz_r.at[d, s, 2 + k])
 
     def weights_split():
         def one(i, carry):
@@ -200,13 +211,8 @@
         kfl[h] = low
         st[h, 0:HD, :] = dot3(split(v_ref[:, cols].T), (high, low), NN)
         st[h, HD:SROWS, :] = jnp.broadcast_to(jnp.sum(kf, axis=0, keepdims=True), (SROWS - HD, FEAT))
-        for n, (start, size) in enumerate(SUBS):
-            rows = pl.ds(start, size)
-            send(st.at[h, rows, :], rr.at[r, rows, :], aa_s.at[h, n], aa_r.at[r, n], (row0 + h, y), r != h)
-
-        @pl.when(r == h)
-        def _():
-            rr[h] = st[h]
+        j = h % 4
+        send(st.at[h], sp.at[j], dd_s.at[j], dd_r.at[j], (other, y), core != h // 4)
 
     def queries(h):
         cols = slice(h * HD, (h + 1) * HD)
@@ -218,50 +224,78 @@
         dl[h] = jnp.broadcast_to(jnp.sum(w, axis=1, keepdims=True), (ROWS, HD))
         nl[h] = dot3(split(w), split(v_ref[:, cols]), NN)
 
-    def row_sums(n):
-        start, size = SUBS[n]
-        rows = pl.ds(start, size)
-        for i in range(1, 8):
-            j = lax.rem(r + i, 8)
-            recv(rr.at[j, rows, :], aa_r.at[j, n])
-        total = jnp.zeros((size, FEAT), F32)
-        for i in range(8):
-            bk[i, start : start + size, :] = total
-            total = total + rr[i, start : start + size, :]
-        zs[start : start + size, :] = total
-
-    def chain(n):
-        start, size = SUBS[n]
-        rows = pl.ds(start, size)
-        recv(zp.at[rows, :], ch_r.at[n], z > 0)
-
-        @pl.when(z == 0)
+    def chip_sum(j):
+        h = 4 * core + j
+        recv(sp.at[j], dd_r.at[j])
+        su[j] = st[h] + sp[j]
+        send(su.at[j], rr.at[x], aa_s.at[j], aa_r.at[x], at(z, j), x != j)
+
+        @pl.when(x == j)
         def _():
-            zp[start : start + size, :] = jnp.zeros((size, FEAT), F32)
-
-        @pl.when(z > 0)
-        def _():
-            zs[start : start + size, :] += zp[start : start + size, :]
-
-        send(zs.at[rows, :], zp.at[rows, :], ch_s.at[n], ch_r.at[n], at(lax.rem(z + 1, NZ), x), z < NZ - 1)
-
-    def send_back(n):
-        start, size = SUBS[n]
-        rows = pl.ds(start, size)
-        before = zp[start : start + size, :]
-        for i in range(8):
-            bk[i, start : start + size, :] += before
-            send(bk.at[i, rows, :], pf.at[r, rows, :], bb_s.at[i, n], bb_r.at[r, n], (row0 + i, y), r != i)
-
-            @pl.when(r == i)
+            rr[j] = su[j]
+
+    def row_sum():
+        for i in range(1, NX):
+            xx = lax.rem(x + i, NX)
+            recv(rr.at[xx], aa_r.at[xx])
+        total = jnp.zeros((SROWS, FEAT), F32)
+        for i in range(NX):
+            bk[i] = total
+            total = total + rr[i]
+        for j in range(NZ):
+            zt[j, 0:PIECE, :] = total[j * PIECE : (j + 1) * PIECE]
+            zt[j, PIECE:, :] = total[HD:]
+        for i in range(1, NZ):
+            zz = lax.rem(z + i, NZ)
+            send(zt.at[zz], zr.at[z], z1_s.at[i - 1], z1_r.at[z], at(zz, x))
+        zr[z] = zt[z]
+
+    def z_sum():
+        for i in range(1, NZ):
+            zz = lax.rem(z + i, NZ)
+            recv(zr.at[zz], z1_r.at[zz])
+        total = jnp.zeros((PIECE, FEAT), F32)
+        norm = jnp.zeros((SROWS - HD, FEAT), F32)
+        for j in range(NZ):
+            zb[j] = total
+            total = total + zr[j, 0:PIECE, :]
+            norm = norm + jnp.where(j < z, zr[j, PIECE:, :], 0.0)
+        rows = pl.ds(pl.multiple_of(z * PIECE, PIECE), PIECE)
+        for i in range(1, NZ):
+            zz = lax.rem(z + i, NZ)
+            send(zb.at[zz], zp.at[rows, :], z2_s.at[i - 1], z2_r.at[z], at(zz, x))
+        zp[rows, :] = zb[z]
+        zp[HD:SROWS, :] = norm
+
+    def send_back():
+        for i in range(1, NZ):
+            zz = lax.rem(z + i, NZ)
+            recv(zp.at[pl.ds(pl.multiple_of(zz * PIECE, PIECE), PIECE), :], z2_r.at[zz])
+        before = zp[...]
+        for i in range(NX):
+            bk[i] += before
+            send(bk.at[i], pc.at[x], bb_s.at[i], bb_r.at[x], at(z, i), x != i)
+
+            @pl.when(x == i)
             def _(i=i):
-                pf[i, start : start + size, :] = bk[i, start : start + size, :]
+                pc[i] = bk[i]
+
+    def cores_prefix():
+        for j in range(4):
+            if j == 0:
+                for i in range(1, NX):
+                    xx = lax.rem(x + i, NX)
+                    recv(pc.at[xx], bb_r.at[xx])
+            h = 4 * core + j
+            low = pc[j]
+            high = low + jnp.where(core == 0, st[h], sp[j])
+            pf[h] = jnp.where(core == 0, low, high)
+            sd[j] = jnp.where(core == 0, high, low)
+            send(sd.at[j], pf.at[h], ee_s.at[j], ee_r.at[j], (other, y))
 
     def prefix_done():
-        for n, (start, size) in enumerate(SUBS):
-            for i in range(1, 8):
-                j = lax.rem(r + i, 8)
-                recv(pf.at[j, pl.ds(start, size), :], bb_r.at[j, n])
+        for j in range(4):
+            recv(pf.at[4 * (1 - core) + j], ee_r.at[j])
 
     def mix(c):
         rows = pl.ds(c * CR, CR)
@@ -325,58 +359,77 @@
                         low_half, pltpu.roll(a, 64, 1), b
                     )
 
-    def ring_step(s):
-        for i in range(NX):
+    def ring_unit(s, i):
+        for d in range(2):
+            ring_x(d, s, i)
+        if i == 0:
             for d in range(2):
-                ring_x(d, s, i)
-            if i == 0:
-                for d in range(2):
-                    ring_z(d, s)
-
-    for h in range(HEADS):
-        keys(h)
-        if h == 1:
-            weights_y_done()
-            weights_x_send()
+                ring_z(d, s)
+        if i == 2:
             for d in range(2):
-                ring_x(d, 0, 0)
-                ring_z(d, 0)
-        if h == 4:
-            for i in range(1, NX):
-                weights_x_done(i)
-                for d in range(2):
-                    ring_x(d, 0, i)
-    for h in range(HEADS):
+                relay_z(d, s - 1)
+
+    units = [(s, i) for s in range(1, 5) for i in range(NX)]
+
+    def advance(n):
+        for _ in range(n):
+            if units:
+                ring_unit(*units.pop(0))
+
+    for j in range(4):
+        keys(j)
+        keys(4 + j)
+        if j > 0:
+            chip_sum(j - 1)
+    chip_sum(3)
+    weights_y_done()
+    weights_x_send()
+    for d in range(2):
+        ring_x(d, 0, 0)
+        ring_z(d, 0)
+    for h in range(4):
         queries(h)
-        if h == 1:
-            ring_step(1)
-        if h == 4:
-            for n in range(len(SUBS)):
-                row_sums(n)
-    for n in range(len(SUBS)):
-        chain(n)
-    ring_step(2)
-    for n in range(len(SUBS)):
-        send_back(n)
-    ring_step(3)
-    ring_step(4)
+    row_sum()
+    for i in range(1, NX):
+        weights_x_done(i)
+        for d in range(2):
+            ring_x(d, 0, i)
+    for h in range(4, HEADS):
+        queries(h)
+    advance(2)
+    z_sum()
+    advance(2)
+    send_back()
+    advance(3)
+    cores_prefix()
+    advance(1)
     prefix_done()
     for c in range(CHUNKS):
         mix(c)
+        advance(1)
+    advance(1)
+    relay(0)
+    advance(2)
+    relay(1)
+    advance(16)
+    for d in range(2):
+        relay_z(d, 4)
+    relay(2)
     for s in range(5):
         for d in range(2):
             ring_z_done(d, s)
     weights_split()
-    relay(0)
     for c in range(CHUNKS):
         project(c)
-        if c + 1 < CHUNKS:
-            relay(c + 1)
-        if c > 0:
-            gather(c - 1)
+        if c == 0:
+            relay(3)
+        if c > 1:
+            gather(c - 2)
+    gather(CHUNKS - 2)
+    for c in range(CHUNKS - 1):
+        finish(c)
     gather(CHUNKS - 1)
-    for c in range(CHUNKS):
-        finish(c)
+    finish(CHUNKS - 1)
     for when, c in pending:
         if when is None:
             c.wait_send()
@@ -386,23 +439,25 @@
 
 def attend(q, k, v, qm, km, wt):
     dma = pltpu.SemaphoreType.DMA
-    subs = len(SUBS)
     vmem = pltpu.VMEM
     scratch = [
         vmem((HEADS, ROWS, FEAT), BF16), vmem((HEADS, ROWS, FEAT), BF16),
         vmem((HEADS, ROWS, FEAT), BF16), vmem((HEADS, ROWS, FEAT), BF16),
         vmem((HEADS, ROWS, HD), F32), vmem((HEADS, ROWS, HD), F32),
-        vmem((HEADS, SROWS, FEAT), F32), vmem((HEADS, SROWS, FEAT), F32),
-        vmem((HEADS, SROWS, FEAT), F32), vmem((HEADS, SROWS, FEAT), F32),
-        vmem((SROWS, FEAT), F32), vmem((SROWS, FEAT), F32),
+        vmem((HEADS, SROWS, FEAT), F32), vmem((4, SROWS, FEAT), F32), vmem((4, SROWS, FEAT), F32),
+        vmem((NX, SROWS, FEAT), F32), vmem((NX, SROWS, FEAT), F32), vmem((NX, SROWS, FEAT), F32),
+        vmem((4, SROWS, FEAT), F32), vmem((HEADS, SROWS, FEAT), F32),
+        vmem((NZ, PIECE + 8, FEAT), F32), vmem((NZ, PIECE + 8, FEAT), F32),
+        vmem((NZ, PIECE, FEAT), F32), vmem((SROWS, FEAT), F32),
         vmem((4, NX, 64, HALF), F32), vmem((1024, HALF), BF16), vmem((1024, HALF), BF16),
         vmem((2, 2, ROWS, WIDTH), F32), vmem((2 * CR, HALF), BF16), vmem((2 * CR, HALF), BF16),
         vmem((CHUNKS, 2 * CR, 512), F32), vmem((CHUNKS, 2 * CR, 512), F32),
         vmem((CHUNKS, 2 * CR, 512), F32), vmem((CHUNKS, CR, 512), F32),
         dma((2, 2)), dma((NY,)), dma((3,)), dma((NX,)),
         dma((2, 4, NX)), dma((2, 4, NX)), dma((2, 4)), dma((2, 4)),
-        dma((2, 5, 3)), dma((2, 5, NX)),
-        dma((8, subs)), dma((8, subs)), dma((subs,)), dma((subs,)), dma((8, subs)), dma((8, subs)),
+        dma((2, 5, 4)), dma((2, 5, 4)),
+        dma((4,)), dma((4,)), dma((4,)), dma((NX,)), dma((NZ - 1,)), dma((NZ,)), dma((NZ - 1,)), dma((NZ,)),
+        dma((4,)), dma((NX,)), dma((4,)), dma((4,)),
         dma((CHUNKS, 3)), dma((CHUNKS, 3)), dma((CHUNKS,)), dma((CHUNKS,)), dma((CHUNKS,)), dma((CHUNKS,)),
     ]
     return pl.pallas_call(

time: 148 us -> 126 us (0.85); the launches traced: 145 us -> 125 us
  Pallas kernels: 143 us -> 123 us
    pallas_call x1, Pallas kernels: 143 us -> 123 us  [attend(): pl.pallas_call(kernel, out_shape=jax.ShapeDtypeStruct((ROWS, WIDTH), F32)...]
where the time goes in v3:
time: 126 us; the launch traced here: 125 us
  Pallas kernels  123 us (98%)
  other arithmetic  2.38 us (2%)
    pallas_call x1, Pallas kernels, attend(): pl.pallas_call(kernel, out_shape=jax.ShapeDtypeStruct((ROWS, WIDTH), F32)...  123 us

profile of v3, /device:TPU:1, one launch (start us, length us, event | category | flops | bytes accessed | tf_op | source)
XLA Modules:
  0.0 125.4 jit_solution(14635023801494454863)
XLA Ops:
  0.0 0.0 copy-start
  0.0 123.0 %shard_map.73 = f32[256,1024]{1,0:T(8,128)} custom-call(f32[256,1024]{1,0:T(8,128)} %q_ref.1, f32[256,1024]{1,0:T(8,128)} %k_ref.1, f32[256,1024]{1,0:T(8,128)} %v_ref.1, f32[8,128,128]{2,1,0:T(8,128)} %qm_ref.1, f32[8,128,128]{2,1,0:T(8,128)} %km_ref.1, f32[16,4096]{1,0:T(8,128)} %bitcast.1), custom_call_target="tpu_custom_call" | custom-call | tf_op jit(solution)/shard_map/pallas_call | solution.py:463
  123.0 0.0 copy-done
  123.0 2.4 %add.3 = f32[256,1024]{1,0:T(8,128)} add(f32[256,1024]{1,0:T(8,128)S(1)} %copy-done, f32[256,1024]{1,0:T(8,128)} %shard_map.73) | non-fusion elementwise | flops 262144 | bytes 3145728 | tf_op jit(solution)/shard_map/add | solution.py:476
Async XLA Ops:
  0.0 123.0 %copy-start = (f32[256,1024]{1,0:T(8,128)S(1)}, f32[256,1024]{1,0:T(8,128)}, u32[]{:S(2)}) copy-start(f32[256,1024]{1,0:T(8,128)} %param.13) | copy-start | bytes 3145732

commit v4 on v3

--- a/solution.py
+++ b/solution.py
@@ -9,7 +9,6 @@
 NX, NY, NZ = 4, 4, 8
 ROWS, HEADS, HD, FEAT = 256, 8, 128, 256
 WIDTH = HEADS * HD
-HALF = 2048
 KP = 1024
 KZ = 512
 KX = KP - KZ
@@ -50,16 +49,13 @@
 def kernel(
     q_ref, k_ref, v_ref, qm_ref, km_ref, wt_ref, out_ref,
     qfh, qfl, kfh, kfl, nl, dl, st, sp, su, rr, bk, pc, sd, pf, zt, zr, zb, zp,
-    wb, wh, wl, ab, ah, al, co, cs, cr, fr,
+    wb, wh, wl, ab, ah, al, co, fr,
     yg_s, yg_r, xa_s, xa_r, zx_s, zx_r, zz_s, zz_r, xz_s, xz_r,
-    dd_s, dd_r, aa_s, aa_r, z1_s, z1_r, z2_s, z2_r, bb_s, bb_r, ee_s, ee_r, m_s, m_r, c_s, c_r, f_s, f_r,
+    dd_s, dd_r, aa_s, aa_r, z1_s, z1_r, z2_s, z2_r, bb_s, bb_r, ee_s, ee_r, m_s, m_r, f_s, f_r,
 ):
     ctx, y = lax.axis_index("ctx"), lax.axis_index("head")
     core, r = lax.rem(ctx, 2), lax.rem(ctx, 8)
     x, z = lax.div(r, 2), lax.div(ctx, 8)
-    yp = lax.rem(y, 2)
-    pair = y + 1 - 2 * yp
-    far = 3 - y
     other = ctx + 1 - 2 * core
     pending = []
 
@@ -86,54 +82,46 @@
         else:
             pl.when(when)(c.wait_recv)
 
-    def member(zz):
-        a = jnp.where(lax.rem(zz + 2, NZ) < 4, 0, 1)
-        return jnp.logical_or(y == a, y == 3 - a)
-
-    def slot(zz):
-        return lax.rem(zz, 2) + jnp.where(lax.div(zz, 2) == y, 0, 2)
-
-    def twin(zz):
-        return zz + 2 - 4 * lax.rem(lax.div(zz, 2), 2)
-
     barrier = pltpu.get_barrier_semaphore()
     greeted = [(ctx, lax.rem(y + i, NY)) for i in range(1, NY)]
     greeted += [at(z, lax.rem(x + i, NX)) for i in range(1, NX)] + [(other, y)]
     greeted += [at(lax.rem(z + i, NZ), x) for i in range(1, NZ)]
-    greeted += [(at(twin(z), x)[0], lax.rem(y + i, NY)) for i in range(1, NY)]
     for device in greeted:
         pl.semaphore_signal(barrier, inc=1, device_id=device, device_id_type=MESH)
-    pl.semaphore_wait(barrier, len(greeted))
-
-    first = jnp.where(lax.rem(z + 2, NZ) < 4, 0, 1)
+    parity, zy = lax.rem(z, 2), lax.div(z, 2)
+    for i in range(NY):
+        to_there = at(2 * i + parity, x)[0]
+
+        @pl.when(jnp.logical_or(i != zy, y != zy))
+        def _(there=to_there):
+            pl.semaphore_signal(barrier, inc=1, device_id=(there, zy), device_id_type=MESH)
+
+        @pl.when(jnp.logical_or(i != y, y != zy))
+        def _(i=i):
+            pl.semaphore_signal(barrier, inc=1, device_id=(at(2 * y + parity, x)[0], i), device_id_type=MESH)
+
+    pl.semaphore_wait(barrier, len(greeted) + jnp.where(y == zy, 6, 8))
+
     my_rows = pl.ds(pl.multiple_of(16 * y, 16), 16)
-    for part in range(2):
-        to = first if part == 0 else 3 - first
-        there = lax.rem(z, 2) + jnp.where(lax.div(z, 2) == to, 0, 2)
-        low = slice(part * HALF, part * HALF + KP)
-        dst = wb.at[there, x, my_rows, pl.ds(KP, KP)]
-        send(wt_ref.at[:, pl.ds(part * HALF + KP, KP)], dst, yg_s.at[part, 1], yg_r.at[y], (at(twin(z), x)[0], to))
-        dst = wb.at[there, x, my_rows, pl.ds(0, KP)]
-        send(wt_ref.at[:, pl.ds(part * HALF, KP)], dst, yg_s.at[part, 0], yg_r.at[y], (ctx, to), to != y)
-
-        @pl.when(to == y)
-        def _(there=there, low=low):
-            wb[there, x, my_rows, 0:KP] = wt_ref[:, low]
+    for i in range(NY):
+        cols = pl.ds(i * KP, KP)
+        away = jnp.logical_or(i != zy, y != zy)
+        dst = wb.at[parity, x, my_rows, cols]
+        send(wt_ref.at[:, cols], dst, yg_s.at[i], yg_r.at[y], (at(2 * i + parity, x)[0], zy), away)
+
+        @pl.when(jnp.logical_not(away))
+        def _(i=i):
+            wb[parity, x, my_rows, i * KP : (i + 1) * KP] = wt_ref[:, i * KP : (i + 1) * KP]
 
     def block_of(zz, xx, start, size):
-        has = member(zz)
-        at_slot = slot(jnp.where(has, zz, twin(zz)))
-        cols = pl.ds(pl.multiple_of(jnp.where(has, start, KP + start), 128), size)
-        return wb.at[at_slot, xx, :, cols]
+        cols = pl.ds(pl.multiple_of(KP * lax.div(zz, 2) + start, 128), size)
+        return wb.at[lax.rem(zz, 2), xx, :, cols]
 
     def weights_y_done():
-        has = member(z)
-        at_slot = slot(jnp.where(has, z, twin(z)))
-        cols = pl.ds(pl.multiple_of(jnp.where(has, 0, KP), 128), KP)
+        cols = pl.ds(pl.multiple_of(KP * zy, KP), KP)
         for i in range(NY):
-            yy = lax.rem(y + i, NY)
-            rows = pl.ds(pl.multiple_of(16 * yy, 16), 16)
-            recv(wb.at[at_slot, x, rows, cols], yg_r.at[yy], jnp.logical_not(has) if i == 0 else None)
+            rows = pl.ds(16 * i, 16)
+            recv(wb.at[parity, x, rows, cols], yg_r.at[i], jnp.logical_or(i != y, y != zy))
 
     def weights_x_send():
         for i in range(1, NX):
@@ -174,6 +162,10 @@
     def beside(k, n=1):
         return lax.rem(x + (n if k == 0 else NX - n), NX)
 
+    def part_of(start, size, k):
+        cut = size // 256 * 128
+        return (start, cut) if k == 0 else (start + cut, size - cut)
+
     def relay_z(d, s):
         if s == 0 and d == 1:
             return
@@ -181,7 +173,7 @@
         start, size = ZHALF[d] if s == 4 else (0, KZ)
         for k in range(2):
             recv(block_of(source, beside(1 - k), start, size), xz_r.at[d, s, k])
-            half = block_of(source, beside(1 - k), start + k * (size // 2), size // 2)
+            half = block_of(source, beside(1 - k), *part_of(start, size, k))
             send(half, half, xz_s.at[d, s, 2 + k], xz_r.at[d, s, 2 + k], at(z, beside(k)))
 
     def ring_z_done(d, s):
@@ -190,18 +182,17 @@
         source = ring(z, 1 - d, s)
         start, size = ZHALF[d] if s == 4 else (0, KZ)
         for k in range(2):
-            recv(block_of(source, beside(1 - k, 2), start + k * (size // 2), size // 2), xz_r.at[d, s, 2 + k])
+            recv(block_of(source, beside(1 - k, 2), *part_of(start, size, k)), xz_r.at[d, s, 2 + k])
 
     def weights_split():
         def one(i, carry):
-            zi, xx = lax.div(i, NX), lax.rem(i, NX)
-            high, low = split(wb[zi, xx])
+            high, low = split(wb[lax.div(i, NX), lax.rem(i, NX)])
             rows = pl.ds(pl.multiple_of(i * 64, 64), 64)
             wh[rows, :] = high
             wl[rows, :] = low
             return carry
 
-        lax.fori_loop(0, 16, one, 0)
+        lax.fori_loop(0, 8, one, 0)
 
     def keys(h):
         cols = slice(h * HD, (h + 1) * HD)
@@ -304,60 +295,64 @@
             qf = (qfh[h, c * CR : (c + 1) * CR, :], qfl[h, c * CR : (c + 1) * CR, :])
             far_sum = dot3(qf, split(state), NT)
             denom = dl[h, c * CR : (c + 1) * CR, :] + far_sum[:, HD : HD + 1]
-            ab[yp, core, rows, h * HD : (h + 1) * HD] = (nl[h, c * CR : (c + 1) * CR, :] + far_sum[:, :HD]) / denom
-        block = ab.at[yp, core, rows, :]
-        send(block, block, m_s.at[c, 0], m_r.at[c, 0], (ctx, pair))
-        send(block, block, m_s.at[c, 1], m_r.at[c, 1], (other, y))
+            ab[y, core, rows, h * HD : (h + 1) * HD] = (nl[h, c * CR : (c + 1) * CR, :] + far_sum[:, :HD]) / denom
+        block = ab.at[y, core, rows, :]
+        for k in range(2):
+            send(block, block, m_s.at[c, k], m_r.at[c, k], (ctx, next_y(k)))
+        send(block, block, m_s.at[c, 2], m_r.at[c, 4], (other, y))
+
+    def next_y(k, n=1):
+        return lax.rem(y + (n if k == 0 else NY - n), NY)
 
     def relay(c):
-        rows = pl.ds(c * CR, CR)
-        block = ab.at[1 - yp, core, rows, :]
-        recv(block, m_r.at[c, 0])
-        send(block, block, m_s.at[c, 2], m_r.at[c, 2], (other, y))
-
-    def project(c):
-        rows = pl.ds(c * CR, CR)
-        recv(ab.at[yp, 1 - core, rows, :], m_r.at[c, 1])
-        recv(ab.at[1 - yp, 1 - core, rows, :], m_r.at[c, 2])
+        for k in range(2):
+            yy = next_y(1 - k)
+            block = ab.at[yy, core, pl.ds(c * CR, CR), :]
+            recv(block, m_r.at[c, k])
+            half = ab.at[yy, core, pl.ds(c * CR + k * (CR // 2), CR // 2), :]
+            send(half, half, m_s.at[c, 3 + k], m_r.at[c, 2 + k], (ctx, next_y(k)))
+            send(block, block, m_s.at[c, 5 + k], m_r.at[c, 5 + k], (other, y))
+
+    def relay_far(c):
+        yy = next_y(0, 2)
+        for k in range(2):
+            recv(ab.at[yy, core, pl.ds(c * CR + k * (CR // 2), CR // 2), :], m_r.at[c, 2 + k])
+        block = ab.at[yy, core, pl.ds(c * CR, CR), :]
+        send(block, block, m_s.at[c, 7], m_r.at[c, 7], (other, y))
+
+    def gather(c):
+        for k, yy in enumerate((y, next_y(1), next_y(0), next_y(0, 2))):
+            recv(ab.at[yy, 1 - core, pl.ds(c * CR, CR), :], m_r.at[c, 4 + k])
         for cc in range(2):
-            for yy in range(2):
+            for yy in range(NY):
                 high, low = split(ab[yy, cc, c * CR : (c + 1) * CR, :])
-                ah[cc * CR : (cc + 1) * CR, yy * WIDTH : (yy + 1) * WIDTH] = high
-                al[cc * CR : (cc + 1) * CR, yy * WIDTH : (yy + 1) * WIDTH] = low
-        for base, dst in ((512, cs), (0, co)):
-
-            def one(n, carry, base=base, dst=dst):
-                wrows = pl.ds(pl.multiple_of(base + n * 256, 256), 256)
-                cols = pl.ds(pl.multiple_of(n * 256, 256), 256)
-                dst[c, :, cols] = dot3((ah[...], al[...]), (wh[wrows, :], wl[wrows, :]), NT)
-                return carry
-
-            lax.fori_loop(0, 2, one, 0)
-            if base:
-                send(cs.at[c], cr.at[c], c_s.at[c], c_r.at[c], (ctx, far))
-
-    def gather(c):
-        recv(cr.at[c], c_r.at[c])
-        co[c] += cr[c]
-        theirs = co.at[c, pl.ds(pl.multiple_of((1 - core) * CR, CR), CR), :]
-        send(theirs, fr.at[c], f_s.at[c], f_r.at[c], (other, y))
-
-    def finish(c):
-        recv(fr.at[c], f_r.at[c])
-        low_half = lax.broadcasted_iota(jnp.int32, (CR, 128), 1) < 64
+                rows, cols = slice(cc * ROWS + c * CR, cc * ROWS + (c + 1) * CR), slice(yy * WIDTH, (yy + 1) * WIDTH)
+                ah[rows, cols] = high
+                al[rows, cols] = low
+
+    def project(n, m):
+        owner = core if m == 0 else 1 - core
+        rows = pl.ds(pl.multiple_of(owner * ROWS, ROWS), ROWS)
+        wrows = slice(n * 256, (n + 1) * 256)
+        co[n, m] = dot3((ah[rows, :], al[rows, :]), (wh[wrows, :], wl[wrows, :]), NT)
+        if m:
+            send(co.at[n, 1], fr.at[n], f_s.at[n], f_r.at[n], (other, y))
+
+    def finish(n):
+        recv(fr.at[n], f_r.at[n])
+        low_half = lax.broadcasted_iota(jnp.int32, (ROWS, 128), 1) < 64
         for cc in range(2):
 
             @pl.when(core == cc)
             def _(cc=cc):
-                for m in range(4):
+                for m in range(2):
                     cols = slice(m * 128, (m + 1) * 128)
-                    a, b = co[c, cc * CR : (cc + 1) * CR, cols], fr[c, :, cols]
+                    a, b = co[n, 0, :, cols], fr[n, :, cols]
                     if cc:
                         a, b = b, a
-                    out_ref[c * CR : (c + 1) * CR, m * 256 : m * 256 + 128] = jnp.where(low_half, a, pltpu.roll(b, 64, 1))
-                    out_ref[c * CR : (c + 1) * CR, m * 256 + 128 : (m + 1) * 256] = jnp.where(
-                        low_half, pltpu.roll(a, 64, 1), b
-                    )
+                    start = n * 512 + m * 256
+                    out_ref[:, start : start + 128] = jnp.where(low_half, a, pltpu.roll(b, 64, 1))
+                    out_ref[:, start + 128 : start + 256] = jnp.where(low_half, pltpu.roll(a, 64, 1), b)
 
     def ring_unit(s, i):
         for d in range(2):
@@ -387,49 +382,55 @@
     for d in range(2):
         ring_x(d, 0, 0)
         ring_z(d, 0)
-    for h in range(4):
+    for h in range(0, 4):
         queries(h)
     row_sum()
+    for h in range(4, 8):
+        queries(h)
+    z_sum()
     for i in range(1, NX):
         weights_x_done(i)
         for d in range(2):
             ring_x(d, 0, i)
-    for h in range(4, HEADS):
-        queries(h)
+    send_back()
     advance(2)
-    z_sum()
-    advance(2)
-    send_back()
-    advance(3)
     cores_prefix()
     advance(1)
     prefix_done()
     for c in range(CHUNKS):
         mix(c)
-        advance(1)
     advance(1)
     relay(0)
     advance(2)
     relay(1)
+    advance(2)
+    relay(2)
+    advance(2)
+    relay(3)
+    advance(1)
+    relay_far(0)
+    advance(1)
+    relay_far(1)
+    gather(0)
+    advance(1)
+    relay_far(2)
+    gather(1)
+    relay_far(3)
     advance(16)
+    gather(2)
     for d in range(2):
         relay_z(d, 4)
-    relay(2)
     for s in range(5):
         for d in range(2):
             ring_z_done(d, s)
+    gather(3)
     weights_split()
-    for c in range(CHUNKS):
-        project(c)
-        if c == 0:
-            relay(3)
-        if c > 1:
-            gather(c - 2)
-    gather(CHUNKS - 2)
-    for c in range(CHUNKS - 1):
-        finish(c)
-    gather(CHUNKS - 1)
-    finish(CHUNKS - 1)
+    for n in range(2):
+        project(n, 1)
+        project(n, 0)
+        if n:
+            finish(0)
+    finish(1)
     for when, c in pending:
         if when is None:
             c.wait_send()
@@ -449,16 +450,15 @@
         vmem((4, SROWS, FEAT), F32), vmem((HEADS, SROWS, FEAT), F32),
         vmem((NZ, PIECE + 8, FEAT), F32), vmem((NZ, PIECE + 8, FEAT), F32),
         vmem((NZ, PIECE, FEAT), F32), vmem((SROWS, FEAT), F32),
-        vmem((4, NX, 64, HALF), F32), vmem((1024, HALF), BF16), vmem((1024, HALF), BF16),
-        vmem((2, 2, ROWS, WIDTH), F32), vmem((2 * CR, HALF), BF16), vmem((2 * CR, HALF), BF16),
-        vmem((CHUNKS, 2 * CR, 512), F32), vmem((CHUNKS, 2 * CR, 512), F32),
-        vmem((CHUNKS, 2 * CR, 512), F32), vmem((CHUNKS, CR, 512), F32),
-        dma((2, 2)), dma((NY,)), dma((3,)), dma((NX,)),
+        vmem((2, NX, 64, NY * WIDTH), F32), vmem((512, NY * WIDTH), BF16), vmem((512, NY * WIDTH), BF16),
+        vmem((NY, 2, ROWS, WIDTH), F32), vmem((2 * ROWS, NY * WIDTH), BF16), vmem((2 * ROWS, NY * WIDTH), BF16),
+        vmem((2, 2, ROWS, 256), F32), vmem((2, ROWS, 256), F32),
+        dma((NY,)), dma((NY,)), dma((3,)), dma((NX,)),
         dma((2, 4, NX)), dma((2, 4, NX)), dma((2, 4)), dma((2, 4)),
         dma((2, 5, 4)), dma((2, 5, 4)),
         dma((4,)), dma((4,)), dma((4,)), dma((NX,)), dma((NZ - 1,)), dma((NZ,)), dma((NZ - 1,)), dma((NZ,)),
         dma((4,)), dma((NX,)), dma((4,)), dma((4,)),
-        dma((CHUNKS, 3)), dma((CHUNKS, 3)), dma((CHUNKS,)), dma((CHUNKS,)), dma((CHUNKS,)), dma((CHUNKS,)),
+        dma((CHUNKS, 8)), dma((CHUNKS, 8)), dma((2,)), dma((2,)),
     ]
     return pl.pallas_call(
         kernel,

time: 126 us -> 113 us (0.90)
  Pallas kernels: 123 us -> 110 us
    pallas_call x1, Pallas kernels: 123 us -> 110 us  [attend(): pl.pallas_call(kernel, out_shape=jax.ShapeDtypeStruct((ROWS, WIDTH), F32)...]
where the time goes in v4:
time: 113 us; the launch traced here: 112 us
  Pallas kernels  110 us (97%)
  other arithmetic  2.38 us (2%)
    pallas_call x1, Pallas kernels, attend(): pl.pallas_call(kernel, out_shape=jax.ShapeDtypeStruct((ROWS, WIDTH), F32)...  110 us
    add x1, other arithmetic, body(): residual + attend(queries, keys, values, query_map, key_map, out_weight.T)  2.38 us

profile of v4, /device:TPU:1, one launch (start us, length us, event | category | flops | bytes accessed | tf_op | source)
XLA Modules:
  0.0 112.3 jit_solution(18289235864179880704)
XLA Ops:
  0.0 0.0 copy-start
  0.0 109.9 %shard_map.73 = f32[256,1024]{1,0:T(8,128)} custom-call(f32[256,1024]{1,0:T(8,128)} %q_ref.1, f32[256,1024]{1,0:T(8,128)} %k_ref.1, f32[256,1024]{1,0:T(8,128)} %v_ref.1, f32[8,128,128]{2,1,0:T(8,128)} %qm_ref.1, f32[8,128,128]{2,1,0:T(8,128)} %km_ref.1, f32[16,4096]{1,0:T(8,128)} %bitcast.1), custom_call_target="tpu_custom_call" | custom-call | tf_op jit(solution)/shard_map/pallas_call | solution.py:463
  109.9 0.0 copy-done
  109.9 2.4 %add.3 = f32[256,1024]{1,0:T(8,128)} add(f32[256,1024]{1,0:T(8,128)S(1)} %copy-done, f32[256,1024]{1,0:T(8,128)} %shard_map.73) | non-fusion elementwise | flops 262144 | bytes 3145728 | tf_op jit(solution)/shard_map/add | solution.py:476
Async XLA Ops:
  0.0 109.9 %copy-start = (f32[256,1024]{1,0:T(8,128)S(1)}, f32[256,1024]{1,0:T(8,128)}, u32[]{:S(2)}) copy-start(f32[256,1024]{1,0:T(8,128)} %param.13) | copy-start | bytes 3145732

commit v5 on v4

--- a/solution.py
+++ b/solution.py
@@ -47,17 +47,23 @@
 
 
 def kernel(
-    q_ref, k_ref, v_ref, qm_ref, km_ref, wt_ref, out_ref,
+    q_in, k_in, v_in, qm_in, km_in, wt_in, res_in, out_ref,
+    q_ref, k_ref, v_ref, qm_ref, km_ref, wt_ref, res_ref,
     qfh, qfl, kfh, kfl, nl, dl, st, sp, su, rr, bk, pc, sd, pf, zt, zr, zb, zp,
     wb, wh, wl, ab, ah, al, co, fr,
     yg_s, yg_r, xa_s, xa_r, zx_s, zx_r, zz_s, zz_r, xz_s, xz_r,
-    dd_s, dd_r, aa_s, aa_r, z1_s, z1_r, z2_s, z2_r, bb_s, bb_r, ee_s, ee_r, m_s, m_r, f_s, f_r,
+    dd_s, dd_r, aa_s, aa_r, z1_s, z1_r, z2_s, z2_r, bb_s, bb_r, ee_s, ee_r, m_s, m_r, f_s, f_r, in_s,
 ):
     ctx, y = lax.axis_index("ctx"), lax.axis_index("head")
     core, r = lax.rem(ctx, 2), lax.rem(ctx, 8)
     x, z = lax.div(r, 2), lax.div(ctx, 8)
     other = ctx + 1 - 2 * core
     pending = []
+    loads = {}
+    inputs = (wt_in, wt_ref), (k_in, k_ref), (km_in, km_ref), (v_in, v_ref), (q_in, q_ref), (qm_in, qm_ref), (res_in, res_ref)
+    for n, (src, dst) in enumerate(inputs):
+        loads[n] = pltpu.make_async_copy(src, dst, in_s.at[n])
+        loads[n].start()
 
     def at(zz, xx):
         return ((zz * NX + xx) * 2 + core, y)
@@ -101,6 +107,8 @@
             pl.semaphore_signal(barrier, inc=1, device_id=(at(2 * y + parity, x)[0], i), device_id_type=MESH)
 
     pl.semaphore_wait(barrier, len(greeted) + jnp.where(y == zy, 6, 8))
+
+    loads[0].wait()
 
     my_rows = pl.ds(pl.multiple_of(16 * y, 16), 16)
     for i in range(NY):
@@ -184,15 +192,25 @@
         for k in range(2):
             recv(block_of(source, beside(1 - k, 2), *part_of(start, size, k)), xz_r.at[d, s, 2 + k])
 
-    def weights_split():
+    def weights_split(zz):
+        cols = pl.ds(pl.multiple_of(KP * lax.div(zz, 2), KP), KP)
+        half = lax.rem(zz, 2)
+
         def one(i, carry):
-            high, low = split(wb[lax.div(i, NX), lax.rem(i, NX)])
-            rows = pl.ds(pl.multiple_of(i * 64, 64), 64)
-            wh[rows, :] = high
-            wl[rows, :] = low
+            high, low = split(wb[half, i, :, cols])
+            rows = pl.ds(pl.multiple_of(half * 256 + i * 64, 64), 64)
+            wh[rows, cols] = high
+            wl[rows, cols] = low
             return carry
 
-        lax.fori_loop(0, 8, one, 0)
+        lax.fori_loop(0, NX, one, 0)
+
+    def weights_done(s):
+        for d in range(2):
+            ring_z_done(d, s)
+        weights_split(ring(z, 0, s))
+        if 0 < s < 4:
+            weights_split(ring(z, 1, s))
 
     def keys(h):
         cols = slice(h * HD, (h + 1) * HD)
@@ -320,22 +338,28 @@
         block = ab.at[yy, core, pl.ds(c * CR, CR), :]
         send(block, block, m_s.at[c, 7], m_r.at[c, 7], (other, y))
 
-    def gather(c):
-        for k, yy in enumerate((y, next_y(1), next_y(0), next_y(0, 2))):
+    def gather(c, places):
+        for k in places:
+            yy = (y, next_y(1), next_y(0), next_y(0, 2))[k]
             recv(ab.at[yy, 1 - core, pl.ds(c * CR, CR), :], m_r.at[c, 4 + k])
-        for cc in range(2):
-            for yy in range(NY):
+            for cc in range(2):
                 high, low = split(ab[yy, cc, c * CR : (c + 1) * CR, :])
-                rows, cols = slice(cc * ROWS + c * CR, cc * ROWS + (c + 1) * CR), slice(yy * WIDTH, (yy + 1) * WIDTH)
+                rows, cols = slice(cc * ROWS + c * CR, cc * ROWS + (c + 1) * CR), pl.ds(pl.multiple_of(yy * WIDTH, WIDTH), WIDTH)
                 ah[rows, cols] = high
                 al[rows, cols] = low
 
-    def project(n, m):
+    def project(n, m, places):
         owner = core if m == 0 else 1 - core
         rows = pl.ds(pl.multiple_of(owner * ROWS, ROWS), ROWS)
         wrows = slice(n * 256, (n + 1) * 256)
-        co[n, m] = dot3((ah[rows, :], al[rows, :]), (wh[wrows, :], wl[wrows, :]), NT)
-        if m:
+        total = None if 0 in places else co[n, m]
+        for k in places:
+            yy = (y, next_y(1), next_y(0), next_y(0, 2))[k]
+            cols = pl.ds(pl.multiple_of(yy * WIDTH, WIDTH), WIDTH)
+            term = dot3((ah[rows, cols], al[rows, cols]), (wh[wrows, cols], wl[wrows, cols]), NT)
+            total = term if total is None else total + term
+        co[n, m] = total
+        if m and 3 in places:
             send(co.at[n, 1], fr.at[n], f_s.at[n], f_r.at[n], (other, y))
 
     def finish(n):
@@ -351,8 +375,10 @@
                     if cc:
                         a, b = b, a
                     start = n * 512 + m * 256
-                    out_ref[:, start : start + 128] = jnp.where(low_half, a, pltpu.roll(b, 64, 1))
-                    out_ref[:, start + 128 : start + 256] = jnp.where(low_half, pltpu.roll(a, 64, 1), b)
+                    cols = slice(start, start + 128)
+                    out_ref[:, cols] = res_ref[:, cols] + jnp.where(low_half, a, pltpu.roll(b, 64, 1))
+                    cols = slice(start + 128, start + 256)
+                    out_ref[:, cols] = res_ref[:, cols] + jnp.where(low_half, pltpu.roll(a, 64, 1), b)
 
     def ring_unit(s, i):
         for d in range(2):
@@ -371,6 +397,8 @@
             if units:
                 ring_unit(*units.pop(0))
 
+    for n in (1, 2, 3):
+        loads[n].wait()
     for j in range(4):
         keys(j)
         keys(4 + j)
@@ -382,6 +410,8 @@
     for d in range(2):
         ring_x(d, 0, 0)
         ring_z(d, 0)
+    for n in (4, 5):
+        loads[n].wait()
     for h in range(0, 4):
         queries(h)
     row_sum()
@@ -397,6 +427,7 @@
     cores_prefix()
     advance(1)
     prefix_done()
+    near, across = (0, 1, 2), (3,)
     for c in range(CHUNKS):
         mix(c)
     advance(1)
@@ -408,26 +439,33 @@
     advance(2)
     relay(3)
     advance(1)
+    gather(0, near)
+    advance(1)
+    gather(1, near)
     relay_far(0)
-    advance(1)
+    advance(2)
+    for s in range(3):
+        weights_done(s)
+    gather(2, near)
     relay_far(1)
-    gather(0)
-    advance(1)
-    relay_far(2)
-    gather(1)
-    relay_far(3)
     advance(16)
-    gather(2)
+    gather(3, near)
     for d in range(2):
         relay_z(d, 4)
-    for s in range(5):
-        for d in range(2):
-            ring_z_done(d, s)
-    gather(3)
-    weights_split()
+    for s in (3, 4):
+        weights_done(s)
+    loads[6].wait()
+    project(0, 1, near)
+    relay_far(2)
+    project(0, 0, near)
+    relay_far(3)
+    project(1, 1, near)
+    project(1, 0, near)
+    for c in range(CHUNKS):
+        gather(c, across)
     for n in range(2):
-        project(n, 1)
-        project(n, 0)
+        project(n, 1, across)
+        project(n, 0, across)
         if n:
             finish(0)
     finish(1)
@@ -438,10 +476,13 @@
             pl.when(when)(c.wait_send)
 
 
-def attend(q, k, v, qm, km, wt):
+def attend(q, k, v, qm, km, wt, res):
     dma = pltpu.SemaphoreType.DMA
     vmem = pltpu.VMEM
+    block = vmem((ROWS, WIDTH), F32)
+    maps = vmem((HEADS, HD, HD), F32)
     scratch = [
+        block, block, block, maps, maps, vmem((16, NY * WIDTH), F32), block,
         vmem((HEADS, ROWS, FEAT), BF16), vmem((HEADS, ROWS, FEAT), BF16),
         vmem((HEADS, ROWS, FEAT), BF16), vmem((HEADS, ROWS, FEAT), BF16),
         vmem((HEADS, ROWS, HD), F32), vmem((HEADS, ROWS, HD), F32),
@@ -459,21 +500,22 @@
         dma((4,)), dma((4,)), dma((4,)), dma((NX,)), dma((NZ - 1,)), dma((NZ,)), dma((NZ - 1,)), dma((NZ,)),
         dma((4,)), dma((NX,)), dma((4,)), dma((4,)),
         dma((CHUNKS, 8)), dma((CHUNKS, 8)), dma((2,)), dma((2,)),
+        dma((7,)),
     ]
     return pl.pallas_call(
         kernel,
         out_shape=jax.ShapeDtypeStruct((ROWS, WIDTH), F32),
-        in_specs=[pl.BlockSpec(memory_space=vmem)] * 6,
+        in_specs=[pl.BlockSpec(memory_space=pl.ANY)] * 7,
         out_specs=pl.BlockSpec(memory_space=vmem),
         scratch_shapes=scratch,
         compiler_params=pltpu.CompilerParams(
             collective_id=0, has_side_effects=True, vmem_limit_bytes=60 * 1024 * 1024
         ),
-    )(q, k, v, qm, km, wt)
+    )(q, k, v, qm, km, wt, res)
 
 
 def body(queries, keys, values, query_map, key_map, out_weight, residual):
-    return residual + attend(queries, keys, values, query_map, key_map, out_weight.T)
+    return attend(queries, keys, values, query_map, key_map, out_weight.T, residual)
 
 
 def solution(mesh):

time: 113 us -> 108 us (0.956)
  Pallas kernels: 110 us -> 106 us
  other arithmetic: 2.38 us -> 0 us
  local copies, waits for them, and re-layouts: 0.01 us -> 2.31 us
    pallas_call x1, Pallas kernels: 110 us -> 106 us  [attend(): pl.pallas_call(kernel, out_shape=jax.ShapeDtypeStruct((ROWS, WIDTH), F32)...]
    add x1 -> x0, other arithmetic: 2.38 us -> none  [body(): residual + attend(queries, keys, values, query_map, key_map, out_weight.T)]
    unnamed x2 -> x1, local copies, waits for them, and re-layouts: 0.01 us -> 2.31 us
where the time goes in v5:
time: 108 us
  Pallas kernels  106 us (98%)
  local copies, waits for them, and re-layouts  2.31 us (2%)
    pallas_call x1, Pallas kernels, attend(): pl.pallas_call(kernel, out_shape=jax.ShapeDtypeStruct((ROWS, WIDTH), F32)...  106 us
    unnamed x1, local copies, waits for them, and re-layouts  2.31 us

profile of v5, /device:TPU:1, one launch (start us, length us, event | category | flops | bytes accessed | tf_op | source)
XLA Modules:
  0.0 107.9 jit_solution(14150300977854874878)
XLA Ops:
  0.0 105.5 %shard_map.73 = f32[256,1024]{1,0:T(8,128)} custom-call(f32[256,1024]{1,0:T(8,128)} %q_in.1, f32[256,1024]{1,0:T(8,128)} %k_in.1, f32[256,1024]{1,0:T(8,128)} %v_in.1, f32[8,128,128]{2,1,0:T(8,128)} %qm_in.1, f32[8,128,128]{2,1,0:T(8,128)} %km_in.1, f32[16,4096]{1,0:T(8,128)} %bitcast.1, f32[256,1024]{1,0:T(8,128)} %res_in.1), custom_call_target="tpu_custom_call" | custom-call | tf_op jit(solution)/shard_map/pallas_call | solution.py:505
  105.5 2.3 %copy.9 = f32[256,1024]{1,0:T(8,128)} copy(f32[256,1024]{1,0:T(8,128)} %shard_map.73) | data formatting | bytes 2097152

commit v6 on v5

--- a/solution.py
+++ b/solution.py
@@ -132,7 +132,7 @@
             recv(wb.at[parity, x, rows, cols], yg_r.at[i], jnp.logical_or(i != y, y != zy))
 
     def weights_x_send():
-        for i in range(1, NX):
+        for i in (1, 3, 2):
             xx = lax.rem(x + i, NX)
             block = block_of(z, x, KZ, KX)
             send(block, block, xa_s.at[i - 1], xa_r.at[x], at(z, xx))
@@ -386,11 +386,11 @@
         if i == 0:
             for d in range(2):
                 ring_z(d, s)
-        if i == 2:
+        if i == 3:
             for d in range(2):
                 relay_z(d, s - 1)
 
-    units = [(s, i) for s in range(1, 5) for i in range(NX)]
+    units = [(s, i) for s in range(1, 5) for i in (0, 1, 3, 2)]
 
     def advance(n):
         for _ in range(n):
@@ -417,13 +417,16 @@
     row_sum()
     for h in range(4, 8):
         queries(h)
+    weights_x_done(1)
+    for d in range(2):
+        ring_x(d, 0, 1)
     z_sum()
-    for i in range(1, NX):
+    for i in (3, 2):
         weights_x_done(i)
         for d in range(2):
             ring_x(d, 0, i)
     send_back()
-    advance(2)
+    advance(3)
     cores_prefix()
     advance(1)
     prefix_done()

time: 108 us -> 104 us (0.963)
  Pallas kernels: 106 us -> 102 us
    pallas_call x1, Pallas kernels: 106 us -> 102 us  [attend(): pl.pallas_call(kernel, out_shape=jax.ShapeDtypeStruct((ROWS, WIDTH), F32)...]
where the time goes in v6:
time: 104 us
  Pallas kernels  102 us (98%)
  local copies, waits for them, and re-layouts  2.31 us (2%)
    pallas_call x1, Pallas kernels, attend(): pl.pallas_call(kernel, out_shape=jax.ShapeDtypeStruct((ROWS, WIDTH), F32)...  102 us
    unnamed x1, local copies, waits for them, and re-layouts  2.31 us

profile of v6, /device:TPU:1, one launch (start us, length us, event | category | flops | bytes accessed | tf_op | source)
XLA Modules:
  0.0 103.9 jit_solution(10353978619338642862)
XLA Ops:
  0.0 101.6 %shard_map.73 = f32[256,1024]{1,0:T(8,128)} custom-call(f32[256,1024]{1,0:T(8,128)} %q_in.1, f32[256,1024]{1,0:T(8,128)} %k_in.1, f32[256,1024]{1,0:T(8,128)} %v_in.1, f32[8,128,128]{2,1,0:T(8,128)} %qm_in.1, f32[8,128,128]{2,1,0:T(8,128)} %km_in.1, f32[16,4096]{1,0:T(8,128)} %bitcast.1, f32[256,1024]{1,0:T(8,128)} %res_in.1), custom_call_target="tpu_custom_call" | custom-call | tf_op jit(solution)/shard_map/pallas_call | solution.py:508
  101.6 2.3 %copy.9 = f32[256,1024]{1,0:T(8,128)} copy(f32[256,1024]{1,0:T(8,128)} %shard_map.73) | data formatting | bytes 2097152
